TPU v7x, 256 devices: a whole 4x4x8 slice. The times are simulated.
256 devices in a mesh: layer: 4 (over z_lo), latent: 64 (over y, z_hi, x, core).
Axes of the slice: x: 4, y: 4, z: 8 (z_hi: 2, z_lo: 4; z = z_hi * 4 + z_lo), core: 2. Of those that a mesh axis runs over, the one named last changes fastest.
Arguments:
- acts: float32 [4, 512, 2304], P('layer', 'latent'), may hold values from -6 to 6
- w_enc: float32 [4, 2304, 16384], P('layer', None, 'latent'), may hold values from -0.0625 to 0.0625
- b_enc: float32 [16384], P('latent'), may hold values from -3 to 3
- w_dec: float32 [16384, 4, 2304], P('latent', 'layer'), may hold values from -0.046875 to 0.046875
- b_dec: float32 [4, 2304], P('layer'), may hold values from -3 to 3
Outputs:
- grad_enc: float32 [4, 2304, 16384], P('layer', None, 'latent')
- grad_benc: float32 [16384], P('latent')
All inputs are finite; a program needn't handle non-finite values.
Results may differ from a plain program's by a relative error of at most 0.000076.
Values sent between devices are 32-bit elements; how exact they have to be, the bound alone decides.
A program may use at most 64 MiB of HBM per device.

v0:
```python
import jax
import jax.numpy as jnp
from jax import lax
from jax.sharding import PartitionSpec as P

SHARP = 4.0


def on_device(acts, w_enc, b_enc, w_dec, b_dec):
    high = lax.Precision.HIGHEST
    encoder = w_enc[0]
    decoder = w_dec[:, 0, :]
    offset = b_dec[0]
    norms = jnp.sqrt(jnp.sum(decoder * decoder, axis=1))
    rows = acts.shape[1]
    count = 1
    width = rows // count
    contract_feat = (((1,), (1,)), ((), ()))
    local = acts[0, 0:width]
    gathered = lax.all_gather(local, "latent", axis=0, tiled=True)
    partial_value = jnp.dot(gathered, encoder, precision=high, preferred_element_type=jnp.float32)
    pre = lax.psum(partial_value, "layer") + b_enc[None, :]
    codes = jax.nn.softplus(SHARP * pre) / SHARP
    recon = lax.psum_scatter(
        jnp.dot(codes, decoder, precision=high, preferred_element_type=jnp.float32),
        "latent",
        scatter_dimension=0,
        tiled=True,
    )
    resid = recon + offset[None, :] - local
    grad_part = lax.dot_general(
        lax.all_gather(resid, "latent", axis=0, tiled=True),
        decoder,
        contract_feat,
        precision=high,
        preferred_element_type=jnp.float32,
    )
    code_grad = lax.psum(grad_part + norms[None, :], "layer")
    pre_grad = code_grad * jax.nn.sigmoid(SHARP * pre)
    grad = lax.dot_general(
        gathered,
        pre_grad,
        (((0,), (0,)), ((), ())),
        precision=high,
        preferred_element_type=jnp.float32,
    )
    grad_bias = jnp.sum(pre_grad, axis=0)
    return (grad[None, :, :], grad_bias)


def solution(mesh):
    return jax.shard_map(
        on_device,
        mesh=mesh,
        in_specs=(
            P("layer", "latent", None),
            P("layer", None, "latent"),
            P("latent"),
            P("latent", "layer", None),
            P("layer", None),
        ),
        out_specs=(P("layer", None, "latent"), P("latent")),
        check_vma=False,
    )
```

profile of v0, /device:TPU:1, one launch (start us, length us, event | category | flops | bytes accessed | tf_op | source)
XLA Modules:
  0.0 510.6 jit_solution(7431164604599933609)
XLA Ops:
  7.2 0.0 all-gather.6.cloned.1.call-start
  7.2 0.7 all-gather.6.cloned.1.call-update
  7.9 0.0 all-reduce.3.cloned.1.call-start
  8.0 102.8 %all-gather.6.cloned.1.call-done = f32[1,512,2304]{2,1,0:T(8,128)} async-done(((f32[1,8,2304]{2,1,0:T(8,128)}), f32[1,512,2304]{2,1,0:T(8,128)}) %all-gather.6.cloned.1.call-update) | async-done | bytes 4718608 | tf_op jit(solution)/shard_map/all_gather | solution.py:20
  110.8 7.0 %fusion.2 = f32[512,256]{1,0:T(8,128)} fusion(f32[1,512,2304]{2,1,0:T(8,128)} %all-gather.6.cloned.1.call-done, f32[1,2304,256]{2,1,0:T(8,128)S(1)} %copy-done), kind=kOutput, calls=%fused_computation.2 | convolution fusion | flops 3623878656 | bytes 7602176 | tf_op jit(solution)/shard_map/dot_general | solution.py:21
  117.8 0.0 all-reduce.3.cloned.1.call-update
  117.8 0.0 reduce-scatter.2.cloned.1.call-start
  117.8 44.0 %all-reduce.3.cloned.1.call-done = f32[512,256]{1,0:T(8,128)} async-done(((f32[512,256]{1,0:T(8,128)}), f32[512,256]{1,0:T(8,128)}) %all-reduce.3.cloned.1.call-update) | async-done | bytes 524304 | tf_op jit(solution)/shard_map/psum | solution.py:22
  161.9 8.3 %fusion.9 = f32[512,2304]{1,0:T(8,128)} fusion(f32[256,1,2304]{2,1,0:T(1,128)} %param.8, f32[512,256]{1,0:T(8,128)} %all-reduce.3.cloned.1.call-done, f32[256]{0:T(256)S(1)} %copy-done.5), kind=kOutput, calls=%fused_computation.8 | convolution fusion | flops 3625058304 | bytes 7603200 | tf_op jit(solution)/shard_map/dot_general | solution.py:25
  170.2 0.0 reduce-scatter.2.cloned.1.call-update
  170.3 0.0 all-gather.4.cloned.1.call-start
  170.3 0.6 copy-done.4
  171.0 173.3 %reduce-scatter.2.cloned.1.call-done = f32[8,2304]{1,0:T(8,128)} async-done(((f32[512,2304]{1,0:T(8,128)}), f32[8,2304]{1,0:T(8,128)}) %reduce-scatter.2.cloned.1.call-update) | async-done | bytes 73744 | tf_op jit(solution)/shard_map/reduce_scatter | solution.py:24
  344.3 1.5 bitcast_subtract_fusion
  345.8 0.0 all-gather.4.cloned.1.call-update
  345.9 0.2 all-reduce.5.cloned.1.call-start
  346.1 1.9 fusion.11
  348.0 92.1 %all-gather.4.cloned.1.call-done = f32[512,2304]{1,0:T(8,128)} async-done(((f32[8,2304]{1,0:T(8,128)}), f32[512,2304]{1,0:T(8,128)}) %all-gather.4.cloned.1.call-update) | async-done | bytes 4718608 | tf_op jit(solution)/shard_map/all_gather | solution.py:32
  440.1 7.8 %fusion.15 = f32[512,256]{1,0:T(8,128)} fusion(f32[512,2304]{1,0:T(8,128)} %all-gather.4.cloned.1.call-done, f32[256,1,2304]{2,1,0:T(1,128)} %param.8, f32[256]{0:T(256)S(1)} %sqrt.7), kind=kOutput, calls=%fused_computation.15 | convolution fusion | flops 3624009728 | bytes 7603200 | tf_op jit(solution)/shard_map/dot_general | solution.py:31
  447.9 0.0 all-reduce.5.cloned.1.call-update
  447.9 44.2 %all-reduce.5.cloned.1.call-done = f32[512,256]{1,0:T(8,128)} async-done(((f32[512,256]{1,0:T(8,128)}), f32[512,256]{1,0:T(8,128)}) %all-reduce.5.cloned.1.call-update) | async-done | bytes 524304 | tf_op jit(solution)/shard_map/psum | solution.py:38
  492.1 8.1 %fusion.4 = f32[1,2304,256]{1,2,0:T(8,128)} fusion(f32[1,512,2304]{2,1,0:T(8,128)} %all-gather.6.cloned.1.call-done, f32[512,256]{1,0:T(8,128)} %all-reduce.5.cloned.1.call-done, f32[512,256]{1,0:T(8,128)S(1)} %copy-done.1, f32[256]{0:T(256)S(1)} %copy-done.5), kind=kOutput, calls=%fused_computation.4 | convolution fusion | flops 3624665088 | bytes 8127488 | tf_op jit(solution)/shard_map/dot_general | solution.py:40
  500.2 3.1 copy.7
  503.3 0.7 fusion.33
  (13 shorter events, 0.1 us)
Async XLA Ops:
  7.2 103.6 %copy-start = (f32[1,2304,256]{2,1,0:T(8,128)S(1)}, f32[1,2304,256]{2,1,0:T(8,128)}, u32[]{:S(2)}) copy-start(f32[1,2304,256]{2,1,0:T(8,128)} %param.6) | copy-start | bytes 7077892
  7.2 103.6 %all-gather.6.cloned.1.call-start = ((), (), s32[]{:S(2)}) async-start(), calls=%async_computation.5 | async-start | bytes 4792320 | tf_op jit(solution)/shard_map/all_gather | solution.py:20
  7.9 154.0 %copy-start.5 = (f32[256]{0:T(256)S(1)}, f32[256]{0:T(256)}, u32[]{:S(2)}) copy-start(f32[256]{0:T(256)} %param.7) | copy-start | bytes 3076
  7.9 154.0 %all-reduce.3.cloned.1.call-start = ((), (), s32[]{:S(2)}) async-start(), calls=%async_computation.1 | async-start | bytes 1048576 | tf_op jit(solution)/shard_map/psum | solution.py:22
  117.8 226.5 %reduce-scatter.2.cloned.1.call-start = ((), (), s32[]{:S(2)}) async-start(), calls=%async_computation.2 | async-start | bytes 4792320 | tf_op jit(solution)/shard_map/reduce_scatter | solution.py:24
  170.2 0.7 copy-start.4
  170.2 174.1 %copy-start.3 = (f32[1,8,2304]{2,1,0:T(8,128)S(1)}, f32[1,8,2304]{2,1,0:T(8,128)}, u32[]{:S(2)}) copy-start(f32[1,8,2304]{2,1,0:T(8,128)} %param.5) | copy-start | bytes 221188
  170.3 269.9 %all-gather.4.cloned.1.call-start = ((), (), s32[]{:S(2)}) async-start(), calls=%async_computation.3 | async-start | bytes 4792320 | tf_op jit(solution)/shard_map/all_gather | solution.py:32
  345.9 146.2 %all-reduce.5.cloned.1.call-start = ((), (), s32[]{:S(2)}) async-start(), calls=%async_computation.4 | async-start | bytes 1048576 | tf_op jit(solution)/shard_map/psum | solution.py:38
  348.0 144.1 %copy-start.1 = (f32[512,256]{1,0:T(8,128)S(1)}, f32[512,256]{1,0:T(8,128)}, u32[]{:S(2)}) copy-start(f32[512,256]{1,0:T(8,128)} %all-reduce.3.cloned.1.call-done) | copy-start | bytes 1572868
  500.2 3.1 copy-start.2
Sparse Core Ops, SparseCore 0:
  11.6 99.1 all-gather.5
  117.9 43.9 all-reduce.2
  170.4 173.8 reduce-scatter.1
  348.3 91.8 all-gather.3
  448.1 43.9 all-reduce.4
where the time goes:
time: 512 us; the launch traced here: 511 us
  waiting for transfers between devices  457 us (89%)
  matrix products  31.2 us (6%)
  between operations  13.8 us (3%)
    reduce_scatter x1, waiting for transfers between devices, on_device(): lax.psum_scatter(jnp.dot(codes, decoder, precision=high, preferred_elemen...  173 us
    all_gather x1, waiting for transfers between devices, on_device(): gathered = lax.all_gather(local, 'latent', axis=0, tiled=True)  103 us
    all_gather x1, waiting for transfers between devices, on_device(): lax.all_gather(resid, 'latent', axis=0, tiled=True)  92.1 us
    psum x1, waiting for transfers between devices, on_device(): code_grad = lax.psum(grad_part + norms[None, :], 'layer')  44.2 us
    psum x1, waiting for transfers between devices, on_device(): pre = lax.psum(partial_value, 'layer') + b_enc[None, :]  44 us
  transfers between devices with their start and end apart: 5, of which 5 were waited for; matrix products, arithmetic and copies ran while one was open for 0% of the time, Pallas kernels for 0%

commit v1 on v0

v1 whole, which is shorter than its diff:
```python
import functools

import jax
import jax.numpy as jnp
from jax import lax
from jax.experimental import pallas as pl
from jax.experimental.pallas import tpu as pltpu
from jax.sharding import PartitionSpec as P

SHARP = 4.0
MESH = pl.DeviceIdType.MESH
F32 = jnp.float32
BF16 = jnp.bfloat16

STEPS = (0, 1, -1, 2)
UNIT = 8
CHUNK = 64


def split(value):
    high = value.astype(BF16)
    return high, (value - high.astype(F32)).astype(BF16)


def softplus_and_sigmoid(pre):
    x = SHARP * pre
    e = jnp.exp(-jnp.abs(x))
    codes = (jnp.maximum(x, 0.0) + jnp.log1p(e)) / SHARP
    inv = 1.0 / (1.0 + e)
    return codes, jnp.where(x >= 0, inv, e * inv)


def kernel(
    acts_hbm,
    wenc_hbm,
    wdec_hbm,
    bdec_ref,
    benc_ref,
    grad_hbm,
    gbias_ref,
    acts,
    acts_sib,
    resid,
    wenc,
    wdec,
    wenc_h,
    wenc_l,
    wdec_h,
    wdec_l,
    bias,
    norms,
    recon,
    row_sum,
    far_a,
    far_b,
    from_up,
    from_down,
    first_in,
    plane_out,
    plane_in,
    part,
    near_in,
    inner_out,
    far_in,
    outer_out,
    sig,
    pg,
    pg_in,
    acts_th,
    acts_tl,
    grad_buf,
    ssem,
    rsem,
    lsem,
):
    layer = lax.axis_index("layer")
    place = lax.axis_index("latent")
    core = lax.rem(place, 2)
    x = lax.rem(place // 2, 4)
    z_hi = lax.rem(place // 8, 2)
    y = place // 16

    def device(dx, dy, dz, dc):
        nx = lax.rem(x + dx + 4, 4)
        ny = lax.rem(y + dy + 4, 4)
        nz = lax.rem(z_hi + dz, 2)
        nc = lax.rem(core + dc, 2)
        return (layer, ((ny * 2 + nz) * 4 + nx) * 2 + nc)

    def first(d):
        return device(d * (1 - core), d * core, 0, 0)

    def second(d):
        return device(d * core, d * (1 - core), 0, 0)

    other_plane = device(0, 0, 1, 0)
    sibling = device(0, 0, 0, 1)
    upper = layer // 2
    inner = lax.rem(layer + upper, 2)
    toward = 1 - 2 * upper
    far = (layer + toward, place)
    near = (layer - toward, place)

    state = {"next": 0}
    sent = []

    def copy_to(src, dst, target, index=None):
        if index is None:
            index = state["next"]
            state["next"] += 1
        return pltpu.make_async_remote_copy(
            src_ref=src,
            dst_ref=dst,
            send_sem=ssem.at[index],
            recv_sem=rsem.at[index],
            device_id=target,
            device_id_type=MESH,
        )

    def send(src, dst, target):
        copy = copy_to(src, dst, target)
        copy.start()
        sent.append(copy)
        return copy

    load_acts = pltpu.make_async_copy(acts_hbm.at[0], acts.at[pl.ds(0, UNIT)], lsem.at[0])
    load_enc = pltpu.make_async_copy(wenc_hbm.at[0], wenc.at[0], lsem.at[1])
    load_dec = pltpu.make_async_copy(wdec_hbm, wdec.at[0], lsem.at[2])
    load_acts.start()
    load_enc.start()
    load_dec.start()

    barrier = pltpu.get_barrier_semaphore()
    partners = [first(1), first(-1), first(2), second(1), second(-1), other_plane, sibling, far]
    for partner in partners:
        pl.semaphore_signal(barrier, inc=1, device_id=partner, device_id_type=MESH)

    @pl.when(inner == 1)
    def _():
        pl.semaphore_signal(barrier, inc=1, device_id=near, device_id_type=MESH)

    pl.semaphore_wait(barrier, len(partners) + inner)

    def row(plane, b, a):
        return ((plane * 4 + b) * 4 + a) * UNIT

    def rows(ref, start, count):
        return ref.at[pl.ds(start, count)]

    def gather_first(ref, plane):
        own = rows(ref, row(plane, 0, 0), UNIT)
        return [
            send(own, rows(ref, row(plane, 0, 2), UNIT), first(1)),
            send(own, rows(ref, row(plane, 0, 1), UNIT), first(-1)),
            send(own, rows(ref, row(plane, 0, 3), UNIT), first(2)),
        ]

    def gather_second(ref, plane):
        half = 2 * UNIT
        own = row(plane, 0, 0)
        up = row(plane, 2, 0)
        down = row(plane, 1, 0)
        up0 = send(rows(ref, own, half), rows(ref, up, half), second(1))
        down1 = send(rows(ref, own + half, half), rows(ref, down + half, half), second(-1))
        up1 = send(rows(ref, own + half, half), rows(ref, up + half, half), second(1))
        down0 = send(rows(ref, own, half), rows(ref, down, half), second(-1))
        return up0, down1, up1, down0

    def gather_forward(ref, plane, copies):
        half = 2 * UNIT
        up0, down1, up1, down0 = copies
        last = row(plane, 3, 0)
        up0.wait_recv()
        fwd0 = send(rows(ref, row(plane, 2, 0), half), rows(ref, last, half), second(1))
        down1.wait_recv()
        fwd1 = send(rows(ref, row(plane, 1, 0) + half, half), rows(ref, last + half, half), second(-1))
        return up1, down0, fwd0, fwd1

    def wait_all(copies):
        for copy in copies:
            copy.wait_recv()

    def start_gather(ref):
        to_plane = send(rows(ref, 0, UNIT), rows(ref, row(1, 0, 0), UNIT), other_plane)
        return to_plane, gather_first(ref, 0)

    def split_weights(slot):
        def enc(i, _):
            at = pl.ds(pl.multiple_of(i * 256, 256), 256)
            high, low = split(wenc[slot, at, :])
            wenc_h[at, slot * 256 : (slot + 1) * 256] = high
            wenc_l[at, slot * 256 : (slot + 1) * 256] = low
            return 0

        lax.fori_loop(0, 9, enc, 0)

    def split_decoder(slot):
        def dec(i, _):
            at = pl.ds(pl.multiple_of(i * 32, 32), 32)
            to = pl.ds(pl.multiple_of(slot * 256 + i * 32, 32), 32)
            high, low = split(wdec[slot, at, :])
            wdec_h[to, :] = high
            wdec_l[to, :] = low
            return 0

        lax.fori_loop(0, 8, dec, 0)
        square = wdec[slot] * wdec[slot]
        total = lax.dot_general(
            jnp.ones((8, square.shape[1]), F32),
            square,
            (((1,), (1,)), ((), ())),
            precision=lax.Precision.HIGHEST,
            preferred_element_type=F32,
        )
        norms[:, slot * 256 : (slot + 1) * 256] = jnp.sqrt(total)

    def product(left, right_h, right_l, dims):
        high, low = split(left)
        count = left.shape[0]
        both = lax.dot_general(jnp.concatenate([high, low], axis=0), right_h, dims, preferred_element_type=F32)
        cross = lax.dot_general(high, right_l, dims, preferred_element_type=F32)
        return both[:count] + (both[count:] + cross)

    def sum_index(phase, chunk):
        return state["sum"] + phase * 3 * (256 // CHUNK) + chunk * 3

    def sum_start(phase, chunk):
        at = pl.ds(chunk * CHUNK, CHUNK)
        index = sum_index(phase, chunk)

        @pl.when(inner == 0)
        def _():
            copy_to(part.at[phase, at], near_in.at[phase, at], far, index).start()

    def sum_middle(phase, chunk):
        at = pl.ds(chunk * CHUNK, CHUNK)
        index = sum_index(phase, chunk)

        @pl.when(inner == 1)
        def _():
            copy_to(part.at[phase, at], near_in.at[phase, at], far, index).wait_recv()
            inner_out[phase, at] = part[phase, at] + near_in[phase, at]
            copy_to(inner_out.at[phase, at], far_in.at[phase, at], far, index + 1).start()

    def sum_finish(phase, chunk):
        at = pl.ds(chunk * CHUNK, CHUNK)
        index = sum_index(phase, chunk)
        copy_to(inner_out.at[phase, at], far_in.at[phase, at], far, index + 1).wait_recv()

        @pl.when(inner == 1)
        def _():
            outer_out[phase, at] = part[phase, at] + far_in[phase, at]
            pltpu.make_async_remote_copy(
                src_ref=outer_out.at[phase, at],
                dst_ref=far_in.at[phase, at],
                send_sem=ssem.at[index + 2],
                recv_sem=rsem.at[index + 1],
                device_id=near,
                device_id_type=MESH,
            ).start()
            inner_out_value = inner_out[phase, at]
            sig[at] = inner_out_value + far_in[phase, at]

        @pl.when(inner == 0)
        def _():
            sig[at] = part[phase, at] + far_in[phase, at]

    def sum_drain(phase, chunk):
        at = pl.ds(chunk * CHUNK, CHUNK)
        index = sum_index(phase, chunk)

        @pl.when(inner == 0)
        def _():
            copy_to(part.at[phase, at], near_in.at[phase, at], far, index).wait_send()

        @pl.when(inner == 1)
        def _():
            copy_to(inner_out.at[phase, at], far_in.at[phase, at], far, index + 1).wait_send()
            copy_to(outer_out.at[phase, at], far_in.at[phase, at], near, index + 2).wait_send()

    state["sum"] = 0
    state["next"] = 2 * 3 * (256 // CHUNK)
    chunks = range(256 // CHUNK)
    plain = (((1,), (0,)), ((), ()))
    turned = (((1,), (1,)), ((), ()))

    load_acts.wait()
    to_plane, own_first = start_gather(acts)
    load_enc.wait()
    swap_enc = send(wenc.at[0], wenc.at[1], sibling)
    load_dec.wait()
    swap_dec = send(wdec.at[0], wdec.at[1], sibling)
    wait_all(own_first)
    own_second = gather_second(acts, 0)
    split_weights(0)
    to_plane.wait_recv()
    other_first = gather_first(acts, 1)
    own_rest = gather_forward(acts, 0, own_second)
    wait_all(other_first)
    other_second = gather_second(acts, 1)
    swap_enc.wait_recv()
    split_weights(1)
    wait_all(own_rest)

    def encode(chunk):
        at = pl.ds(chunk * CHUNK, CHUNK)
        part[0, at] = product(acts[at], wenc_h[...], wenc_l[...], plain)
        sum_start(0, chunk)

    encode(0)
    other_rest = gather_forward(acts, 1, other_second)
    encode(1)
    sum_middle(0, 0)
    sum_middle(0, 1)
    wait_all(other_rest)
    encode(2)
    encode(3)
    give_acts = send(acts, acts_sib, sibling)
    split_decoder(0)
    swap_dec.wait_recv()
    split_decoder(1)
    sum_middle(0, 2)
    sum_middle(0, 3)

    bias_row = bias
    bias_row[:, 0:256] = benc_ref[0:1, :]
    swap_bias = send(bias.at[:, pl.ds(0, 256)], bias.at[:, pl.ds(256, 256)], sibling)
    swap_bias.wait_recv()

    def decode(chunk):
        at = pl.ds(chunk * CHUNK, CHUNK)
        sum_finish(0, chunk)
        codes, gate = softplus_and_sigmoid(sig[at] + bias[...])
        sig[at] = gate
        high, low = split(codes)
        both = jnp.concatenate([high, low], axis=0)
        for block in range(3):
            cols = slice(block * 768, (block + 1) * 768)
            main = jnp.dot(both, wdec_h[:, cols], preferred_element_type=F32)
            cross = jnp.dot(high, wdec_l[:, cols], preferred_element_type=F32)
            recon[at, cols] = main[:CHUNK] + (main[CHUNK:] + cross)

    half = 2 * UNIT

    def scatter_start(plane):
        base = row(plane, 3, 0)
        a = send(rows(recon, base, half), far_a.at[plane], second(1))
        b = send(rows(recon, base + half, half), far_b.at[plane], second(-1))
        up1 = send(rows(recon, row(plane, 1, 0) + half, half), from_down.at[plane, pl.ds(half, half)], second(1))
        down0 = send(rows(recon, row(plane, 2, 0), half), from_up.at[plane, pl.ds(0, half)], second(-1))
        return a, b, up1, down0

    def scatter_add(plane, copies):
        a, b, up1, down0 = copies
        to_up = pl.ds(row(plane, 1, 0), half)
        to_down = pl.ds(row(plane, 2, 0) + half, half)
        a.wait_recv()
        recon[to_up] = recon[to_up] + far_a[plane]
        up0 = send(recon.at[to_up], from_down.at[plane, pl.ds(0, half)], second(1))
        b.wait_recv()
        recon[to_down] = recon[to_down] + far_b[plane]
        down1 = send(recon.at[to_down], from_up.at[plane, pl.ds(half, half)], second(-1))
        return up1, down0, up0, down1

    def scatter_first(plane, copies):
        wait_all(copies)
        row_sum[plane] = recon[pl.ds(row(plane, 0, 0), 4 * UNIT)] + (from_up[plane] + from_down[plane])
        return [
            send(row_sum.at[plane, pl.ds(UNIT, UNIT)], first_in.at[plane, 0], first(1)),
            send(row_sum.at[plane, pl.ds(2 * UNIT, UNIT)], first_in.at[plane, 1], first(-1)),
            send(row_sum.at[plane, pl.ds(3 * UNIT, UNIT)], first_in.at[plane, 2], first(2)),
        ]

    def scatter_total(plane, copies):
        wait_all(copies)
        return row_sum[plane, 0:UNIT] + (first_in[plane, 0] + (first_in[plane, 1] + first_in[plane, 2]))

    decode(0)
    decode(1)
    own_scatter = scatter_start(0)
    decode(2)
    own_scatter = scatter_add(0, own_scatter)
    decode(3)
    other_scatter = scatter_start(1)
    own_scatter = scatter_first(0, own_scatter)
    other_scatter = scatter_add(1, other_scatter)
    other_scatter = scatter_first(1, other_scatter)
    own_total = scatter_total(0, own_scatter)
    plane_out[...] = scatter_total(1, other_scatter)
    to_home = send(plane_out, plane_in, other_plane)
    to_home.wait_recv()
    resid[0:UNIT, :] = (own_total + plane_in[...]) + bdec_ref[...] - acts[0:UNIT, :]

    to_plane, own_first = start_gather(resid)
    wait_all(own_first)
    own_second = gather_second(resid, 0)
    to_plane.wait_recv()
    other_first = gather_first(resid, 1)
    own_rest = gather_forward(resid, 0, own_second)
    wait_all(other_first)
    other_second = gather_second(resid, 1)
    wait_all(own_rest)

    def code_gradient(chunk):
        at = pl.ds(chunk * CHUNK, CHUNK)
        part[1, at] = product(resid[at], wdec_h[...], wdec_l[...], turned) + norms[0:1, :]
        sum_start(1, chunk)

    pre_sig = pg
    pre_sig[...] = sig[...]
    code_gradient(0)
    other_rest = gather_forward(resid, 1, other_second)
    code_gradient(1)
    sum_middle(1, 0)
    sum_middle(1, 1)
    wait_all(other_rest)
    code_gradient(2)
    code_gradient(3)

    give_acts.wait_recv()

    def turn(i, _):
        cols = pl.ds(pl.multiple_of(i * 256, 256), 256)
        for half_at, ref in ((0, acts), (256, acts_sib)):
            high, low = split(jnp.transpose(ref[:, cols]))
            acts_th[cols, half_at : half_at + 256] = high
            acts_tl[cols, half_at : half_at + 256] = low
        return 0

    lax.fori_loop(0, 9, turn, 0)

    sum_middle(1, 2)
    sum_middle(1, 3)
    gives = []
    for chunk in chunks:
        at = pl.ds(chunk * CHUNK, CHUNK)
        sum_finish(1, chunk)
        pg[at] = pg[at] * sig[at]
        gives.append(send(pg.at[at, pl.ds(256, 256)], pg_in.at[at], sibling))
    wait_all(gives)

    mine = pg[:, 0:256]
    theirs = pg_in[...]
    gbias_ref[...] = jnp.sum(mine, axis=0, keepdims=True) + jnp.sum(theirs, axis=0, keepdims=True)
    right_h, right_l = split(jnp.concatenate([mine, theirs], axis=0))

    stores = []
    for i in range(9):
        at = pl.ds(i * 256, 256)
        high = acts_th[at, :]
        main = jnp.dot(high, right_h, preferred_element_type=F32)
        cross = jnp.dot(high, right_l, preferred_element_type=F32) + jnp.dot(
            acts_tl[at, :], right_h, preferred_element_type=F32
        )
        grad_buf[at, :] = main + cross
        store = pltpu.make_async_copy(grad_buf.at[at], grad_hbm.at[0, at], lsem.at[3 + i])
        store.start()
        stores.append(store)

    for copy in sent:
        copy.wait_send()
    for phase in range(2):
        for chunk in chunks:
            sum_drain(phase, chunk)
    for store in stores:
        store.wait()


def on_device(acts, w_enc, b_enc, w_dec, b_dec):
    depth = acts.shape[2]
    w_dec = w_dec.reshape(256, depth)
    any_space = pl.BlockSpec(memory_space=pl.ANY)
    vmem = pl.BlockSpec(memory_space=pltpu.VMEM)
    copies = 110
    grad, bias = pl.pallas_call(
        kernel,
        out_shape=(
            jax.ShapeDtypeStruct((1, depth, 256), F32),
            jax.ShapeDtypeStruct((1, 256), F32),
        ),
        in_specs=[any_space, any_space, any_space, vmem, vmem],
        out_specs=(any_space, vmem),
        scratch_shapes=[
            pltpu.VMEM((256, depth), F32),
            pltpu.VMEM((256, depth), F32),
            pltpu.VMEM((256, depth), F32),
            pltpu.VMEM((2, depth, 256), F32),
            pltpu.VMEM((2, 256, depth), F32),
            pltpu.VMEM((depth, 512), BF16),
            pltpu.VMEM((depth, 512), BF16),
            pltpu.VMEM((512, depth), BF16),
            pltpu.VMEM((512, depth), BF16),
            pltpu.VMEM((1, 512), F32),
            pltpu.VMEM((8, 512), F32),
            pltpu.VMEM((256, depth), F32),
            pltpu.VMEM((2, 32, depth), F32),
            pltpu.VMEM((2, 16, depth), F32),
            pltpu.VMEM((2, 16, depth), F32),
            pltpu.VMEM((2, 32, depth), F32),
            pltpu.VMEM((2, 32, depth), F32),
            pltpu.VMEM((2, 3, 8, depth), F32),
            pltpu.VMEM((8, depth), F32),
            pltpu.VMEM((8, depth), F32),
            pltpu.VMEM((2, 256, 512), F32),
            pltpu.VMEM((2, 256, 512), F32),
            pltpu.VMEM((2, 256, 512), F32),
            pltpu.VMEM((2, 256, 512), F32),
            pltpu.VMEM((2, 256, 512), F32),
            pltpu.VMEM((256, 512), F32),
            pltpu.VMEM((256, 512), F32),
            pltpu.VMEM((256, 256), F32),
            pltpu.VMEM((depth, 512), BF16),
            pltpu.VMEM((depth, 512), BF16),
            pltpu.VMEM((depth, 256), F32),
            pltpu.SemaphoreType.DMA((copies,)),
            pltpu.SemaphoreType.DMA((copies,)),
            pltpu.SemaphoreType.DMA((12,)),
        ],
        compiler_params=pltpu.CompilerParams(
            collective_id=0, has_side_effects=True, vmem_limit_bytes=60 * 1024 * 1024
        ),
        cost_estimate=pl.CostEstimate(flops=7_300_000_000, bytes_accessed=10_000_000, transcendentals=500_000),
        name="crosscoder_gradient",
    )(acts, w_enc, w_dec, b_dec, b_enc.reshape(1, 256))
    return grad, bias.reshape(256)


def solution(mesh):
    return jax.shard_map(
        on_device,
        mesh=mesh,
        in_specs=(
            P("layer", "latent", None),
            P("layer", None, "latent"),
            P("latent"),
            P("latent", "layer", None),
            P("layer", None),
        ),
        out_specs=(P("layer", None, "latent"), P("latent")),
        check_vma=False,
    )
```

time: 512 us -> 133 us (0.26)
  waiting for transfers between devices: 457 us -> 0 us
  Pallas kernels: 0 us -> 125 us
  matrix products: 31.2 us -> 0 us
  between operations: 13.8 us -> 0.65 us
    all_gather x2 -> x0, waiting for transfers between devices: 195 us -> none  [the longest x1 103 us: on_device(): gathered = lax.all_gather(local, 'latent', axis=0, tiled=True)]
    reduce_scatter x1 -> x0, waiting for transfers between devices: 173 us -> none  [on_device(): lax.psum_scatter(jnp.dot(codes, decoder, precision=high, preferred_elemen...]
    pallas_call x0 -> x1, Pallas kernels: none -> 125 us  [on_device(): pl.pallas_call(kernel, out_shape=(jax.ShapeDtypeStruct((1, depth, 256), F...]
    psum x2 -> x0, waiting for transfers between devices: 88.2 us -> none  [the longest x1 44.2 us: on_device(): code_grad = lax.psum(grad_part + norms[None, :], 'layer')]
    dot_general x4 -> x0, matrix products: 31.2 us -> none  [the longest x1 8.34 us: on_device(): jnp.dot(codes, decoder, precision=high, preferred_element_type=jnp.float32)]
  transfers between devices with their start and end apart: 5 -> 0, of which waited for: 5 -> 0; matrix products, arithmetic and copies ran while one was open for 0% -> 0% of each run, Pallas kernels for 0% -> 0%
where the time goes in v1:
time: 133 us
  Pallas kernels  125 us (94%)
  local copies, waits for them, and re-layouts  7.01 us (5%)
    pallas_call x1, Pallas kernels, on_device(): pl.pallas_call(kernel, out_shape=(jax.ShapeDtypeStruct((1, depth, 256), F...  125 us
    unnamed x5, local copies, waits for them, and re-layouts  7.01 us

profile of v1, /device:TPU:1, one launch (start us, length us, event | category | flops | bytes accessed | tf_op | source)
XLA Modules:
  0.0 133.1 jit_solution(4629096135791821958)
XLA Ops:
  0.6 3.2 %copy.9 = f32[256,1,2304]{2,0,1:T(8,128)} copy(f32[256,1,2304]{2,1,0:T(1,128)} %param.8) | data formatting | bytes 4718592
  3.9 125.5 %crosscoder_gradient.1 = (f32[1,2304,256]{2,1,0:T(8,128)}, f32[1,256]{1,0:T(1,128)}) custom-call(f32[1,8,2304]{2,1,0:T(8,128)} %acts_hbm.1, f32[1,2304,256]{2,1,0:T(8,128)} %wenc_hbm.1, f32[256,2304]{1,0:T(8,128)} %bitcast.5, f32[1,2304]{1,0:T(1,128)} %bdec_ref.1, f32[1,256]{1,0:T(1,128)} %bitcast.7), custom_call_target="tpu_custom_call" | custom-call | flops 7299999744 | bytes 10000000 | tf_op jit(solution)/shard_map/crosscoder_gradient/pallas_call | solution.py:475
  129.3 0.0 copy-start
  129.4 3.2 %copy.12 = f32[1,2304,256]{2,1,0:T(8,128)} copy(f32[1,2304,256]{2,1,0:T(8,128)} %get-tuple-element.8) | data formatting | bytes 4718592
  132.6 0.0 copy-done
  132.6 0.6 copy.13
Async XLA Ops:
  129.3 3.2 %copy-start = (f32[1,256]{1,0:T(1,128)S(1)}, f32[1,256]{1,0:T(1,128)}, u32[]{:S(2)}) copy-start(f32[1,256]{1,0:T(1,128)} %get-tuple-element.5) | copy-start | bytes 3076

commit v2 on v1

--- a/solution.py
+++ b/solution.py
@@ -125,7 +125,7 @@
 
     load_acts = pltpu.make_async_copy(acts_hbm.at[0], acts.at[pl.ds(0, UNIT)], lsem.at[0])
     load_enc = pltpu.make_async_copy(wenc_hbm.at[0], wenc.at[0], lsem.at[1])
-    load_dec = pltpu.make_async_copy(wdec_hbm, wdec.at[0], lsem.at[2])
+    load_dec = pltpu.make_async_copy(wdec_hbm.at[:, 0], wdec.at[0], lsem.at[2])
     load_acts.start()
     load_enc.start()
     load_dec.start()
@@ -290,16 +290,18 @@
     swap_enc = send(wenc.at[0], wenc.at[1], sibling)
     load_dec.wait()
     swap_dec = send(wdec.at[0], wdec.at[1], sibling)
+    bias[:, 0:256] = benc_ref[0:1, :]
+    swap_bias = send(bias.at[:, pl.ds(0, 256)], bias.at[:, pl.ds(256, 256)], sibling)
     wait_all(own_first)
     own_second = gather_second(acts, 0)
     split_weights(0)
     to_plane.wait_recv()
     other_first = gather_first(acts, 1)
     own_rest = gather_forward(acts, 0, own_second)
+    swap_enc.wait_recv()
+    split_weights(1)
     wait_all(other_first)
     other_second = gather_second(acts, 1)
-    swap_enc.wait_recv()
-    split_weights(1)
     wait_all(own_rest)
 
     def encode(chunk):
@@ -308,24 +310,20 @@
         sum_start(0, chunk)
 
     encode(0)
+    encode(1)
+    split_decoder(0)
     other_rest = gather_forward(acts, 1, other_second)
-    encode(1)
     sum_middle(0, 0)
     sum_middle(0, 1)
+    swap_dec.wait_recv()
+    split_decoder(1)
     wait_all(other_rest)
     encode(2)
     encode(3)
     give_acts = send(acts, acts_sib, sibling)
-    split_decoder(0)
-    swap_dec.wait_recv()
-    split_decoder(1)
+    swap_bias.wait_recv()
     sum_middle(0, 2)
     sum_middle(0, 3)
-
-    bias_row = bias
-    bias_row[:, 0:256] = benc_ref[0:1, :]
-    swap_bias = send(bias.at[:, pl.ds(0, 256)], bias.at[:, pl.ds(256, 256)], sibling)
-    swap_bias.wait_recv()
 
     def decode(chunk):
         at = pl.ds(chunk * CHUNK, CHUNK)
@@ -385,39 +383,15 @@
     own_scatter = scatter_first(0, own_scatter)
     other_scatter = scatter_add(1, other_scatter)
     other_scatter = scatter_first(1, other_scatter)
-    own_total = scatter_total(0, own_scatter)
-    plane_out[...] = scatter_total(1, other_scatter)
-    to_home = send(plane_out, plane_in, other_plane)
-    to_home.wait_recv()
-    resid[0:UNIT, :] = (own_total + plane_in[...]) + bdec_ref[...] - acts[0:UNIT, :]
-
-    to_plane, own_first = start_gather(resid)
-    wait_all(own_first)
-    own_second = gather_second(resid, 0)
-    to_plane.wait_recv()
-    other_first = gather_first(resid, 1)
-    own_rest = gather_forward(resid, 0, own_second)
-    wait_all(other_first)
-    other_second = gather_second(resid, 1)
-    wait_all(own_rest)
-
-    def code_gradient(chunk):
-        at = pl.ds(chunk * CHUNK, CHUNK)
-        part[1, at] = product(resid[at], wdec_h[...], wdec_l[...], turned) + norms[0:1, :]
-        sum_start(1, chunk)
-
-    pre_sig = pg
-    pre_sig[...] = sig[...]
-    code_gradient(0)
-    other_rest = gather_forward(resid, 1, other_second)
-    code_gradient(1)
-    sum_middle(1, 0)
-    sum_middle(1, 1)
-    wait_all(other_rest)
-    code_gradient(2)
-    code_gradient(3)
-
-    give_acts.wait_recv()
+    plane_out[0] = scatter_total(0, own_scatter)
+    own_to_plane = send(plane_out.at[0], plane_in.at[0], other_plane)
+    other_total = scatter_total(1, other_scatter)
+    plane_out[1] = other_total
+    other_to_plane = send(plane_out.at[1], plane_in.at[1], other_plane)
+
+    def residual(plane, total):
+        at = pl.ds(row(plane, 0, 0), UNIT)
+        resid[at] = total + bdec_ref[...] - acts[at]
 
     def turn(i, _):
         cols = pl.ds(pl.multiple_of(i * 256, 256), 256)
@@ -427,12 +401,42 @@
             acts_tl[cols, half_at : half_at + 256] = low
         return 0
 
-    lax.fori_loop(0, 9, turn, 0)
-
+    own_to_plane.wait_recv()
+    residual(1, other_total + plane_in[0])
+    other_first = gather_first(resid, 1)
+    give_acts.wait_recv()
+    lax.fori_loop(0, 4, turn, 0)
+    wait_all(other_first)
+    other_second = gather_second(resid, 1)
+    lax.fori_loop(4, 6, turn, 0)
+    other_to_plane.wait_recv()
+    residual(0, plane_out[0] + plane_in[1])
+    own_first = gather_first(resid, 0)
+    other_rest = gather_forward(resid, 1, other_second)
+    lax.fori_loop(6, 9, turn, 0)
+    wait_all(own_first)
+    own_second = gather_second(resid, 0)
+    wait_all(other_rest)
+
+    def code_gradient(chunk):
+        at = pl.ds(chunk * CHUNK, CHUNK)
+        part[1, at] = product(resid[at], wdec_h[...], wdec_l[...], turned) + norms[0:1, :]
+        sum_start(1, chunk)
+
+    pre_sig = pg
+    pre_sig[...] = sig[...]
+    code_gradient(2)
+    code_gradient(3)
+    own_rest = gather_forward(resid, 0, own_second)
     sum_middle(1, 2)
     sum_middle(1, 3)
+    wait_all(own_rest)
+    code_gradient(0)
+    code_gradient(1)
+    sum_middle(1, 0)
+    sum_middle(1, 1)
     gives = []
-    for chunk in chunks:
+    for chunk in (2, 3, 0, 1):
         at = pl.ds(chunk * CHUNK, CHUNK)
         sum_finish(1, chunk)
         pg[at] = pg[at] * sig[at]
@@ -468,7 +472,6 @@
 
 def on_device(acts, w_enc, b_enc, w_dec, b_dec):
     depth = acts.shape[2]
-    w_dec = w_dec.reshape(256, depth)
     any_space = pl.BlockSpec(memory_space=pl.ANY)
     vmem = pl.BlockSpec(memory_space=pltpu.VMEM)
     copies = 110
@@ -499,8 +502,8 @@
             pltpu.VMEM((2, 32, depth), F32),
             pltpu.VMEM((2, 32, depth), F32),
             pltpu.VMEM((2, 3, 8, depth), F32),
-            pltpu.VMEM((8, depth), F32),
-            pltpu.VMEM((8, depth), F32),
+            pltpu.VMEM((2, 8, depth), F32),
+            pltpu.VMEM((2, 8, depth), F32),
             pltpu.VMEM((2, 256, 512), F32),
             pltpu.VMEM((2, 256, 512), F32),
             pltpu.VMEM((2, 256, 512), F32),

time: 133 us -> 126 us (0.947)
  local copies, waits for them, and re-layouts: 7.01 us -> 3.79 us
  Pallas kernels: 125 us -> 122 us
    pallas_call x1, Pallas kernels: 125 us -> 122 us  [on_device(): pl.pallas_call(kernel, out_shape=(jax.ShapeDtypeStruct((1, depth, 256), F...]
    unnamed x5 -> x4, local copies, waits for them, and re-layouts: 7.01 us -> 3.79 us
where the time goes in v2:
time: 126 us
  Pallas kernels  122 us (97%)
  local copies, waits for them, and re-layouts  3.79 us (3%)
    pallas_call x1, Pallas kernels, on_device(): pl.pallas_call(kernel, out_shape=(jax.ShapeDtypeStruct((1, depth, 256), F...  122 us
    unnamed x4, local copies, waits for them, and re-layouts  3.79 us

profile of v2, /device:TPU:1, one launch (start us, length us, event | category | flops | bytes accessed | tf_op | source)
XLA Modules:
  0.0 126.0 jit_solution(106973555272462669)
XLA Ops:
  0.6 121.6 %crosscoder_gradient.1 = (f32[1,2304,256]{2,1,0:T(8,128)}, f32[1,256]{1,0:T(1,128)}) custom-call(f32[1,8,2304]{2,1,0:T(8,128)} %acts_hbm.1, f32[1,2304,256]{2,1,0:T(8,128)} %wenc_hbm.1, f32[256,1,2304]{2,1,0:T(1,128)} %wdec_hbm.1, f32[1,2304]{1,0:T(1,128)} %bdec_ref.1, f32[1,256]{1,0:T(1,128)} %bitcast.3), custom_call_target="tpu_custom_call" | custom-call | flops 7299999744 | bytes 10000000 | tf_op jit(solution)/shard_map/crosscoder_gradient/pallas_call | solution.py:478
  122.2 0.0 copy-start
  122.2 3.2 %copy.9 = f32[1,2304,256]{2,1,0:T(8,128)} copy(f32[1,2304,256]{2,1,0:T(8,128)} %get-tuple-element.8) | data formatting | bytes 4718592
  125.5 0.0 copy-done
  125.5 0.6 copy.10
Async XLA Ops:
  122.2 3.2 %copy-start = (f32[1,256]{1,0:T(1,128)S(1)}, f32[1,256]{1,0:T(1,128)}, u32[]{:S(2)}) copy-start(f32[1,256]{1,0:T(1,128)} %get-tuple-element.5) | copy-start | bytes 3076

commit v3 on v2

--- a/solution.py
+++ b/solution.py
@@ -14,7 +14,7 @@
 
 STEPS = (0, 1, -1, 2)
 UNIT = 8
-CHUNK = 64
+CHUNKS = ((0, 32), (32, 64), (96, 32), (128, 32), (160, 64), (224, 32))
 
 
 def split(value):
@@ -204,10 +204,13 @@
             return 0
 
         lax.fori_loop(0, 8, dec, 0)
-        square = wdec[slot] * wdec[slot]
+        squares = jnp.zeros((256, 128), F32)
+        for k in range(wdec.shape[2] // 128):
+            value = wdec[slot, :, k * 128 : (k + 1) * 128]
+            squares = squares + value * value
         total = lax.dot_general(
-            jnp.ones((8, square.shape[1]), F32),
-            square,
+            jnp.ones((8, 128), F32),
+            squares,
             (((1,), (1,)), ((), ())),
             precision=lax.Precision.HIGHEST,
             preferred_element_type=F32,
@@ -221,135 +224,110 @@
         cross = lax.dot_general(high, right_l, dims, preferred_element_type=F32)
         return both[:count] + (both[count:] + cross)
 
-    def sum_index(phase, chunk):
-        return state["sum"] + phase * 3 * (256 // CHUNK) + chunk * 3
+    def sum_place(phase, chunk):
+        start, count = CHUNKS[chunk]
+        return pl.ds(start, count), (phase * len(CHUNKS) + chunk) * 3
+
+    def sum_in(phase, chunk):
+        at, index = sum_place(phase, chunk)
+        return copy_to(part.at[phase, at], near_in.at[phase, at], far, index)
+
+    def sum_swap(phase, chunk):
+        at, index = sum_place(phase, chunk)
+        return copy_to(inner_out.at[phase, at], far_in.at[phase, at], far, index + 1)
+
+    def sum_out(phase, chunk):
+        at, index = sum_place(phase, chunk)
+        return pltpu.make_async_remote_copy(
+            src_ref=outer_out.at[phase, at],
+            dst_ref=far_in.at[phase, at],
+            send_sem=ssem.at[index + 2],
+            recv_sem=rsem.at[index + 1],
+            device_id=near,
+            device_id_type=MESH,
+        )
 
     def sum_start(phase, chunk):
-        at = pl.ds(chunk * CHUNK, CHUNK)
-        index = sum_index(phase, chunk)
-
         @pl.when(inner == 0)
         def _():
-            copy_to(part.at[phase, at], near_in.at[phase, at], far, index).start()
+            sum_in(phase, chunk).start()
 
     def sum_middle(phase, chunk):
-        at = pl.ds(chunk * CHUNK, CHUNK)
-        index = sum_index(phase, chunk)
+        at, _ = sum_place(phase, chunk)
 
         @pl.when(inner == 1)
         def _():
-            copy_to(part.at[phase, at], near_in.at[phase, at], far, index).wait_recv()
+            sum_in(phase, chunk).wait_recv()
             inner_out[phase, at] = part[phase, at] + near_in[phase, at]
-            copy_to(inner_out.at[phase, at], far_in.at[phase, at], far, index + 1).start()
-
-    def sum_finish(phase, chunk):
-        at = pl.ds(chunk * CHUNK, CHUNK)
-        index = sum_index(phase, chunk)
-        copy_to(inner_out.at[phase, at], far_in.at[phase, at], far, index + 1).wait_recv()
+            sum_swap(phase, chunk).start()
+
+    def sum_relay(phase, chunk):
+        at, _ = sum_place(phase, chunk)
 
         @pl.when(inner == 1)
         def _():
+            sum_swap(phase, chunk).wait_recv()
             outer_out[phase, at] = part[phase, at] + far_in[phase, at]
-            pltpu.make_async_remote_copy(
-                src_ref=outer_out.at[phase, at],
-                dst_ref=far_in.at[phase, at],
-                send_sem=ssem.at[index + 2],
-                recv_sem=rsem.at[index + 1],
-                device_id=near,
-                device_id_type=MESH,
-            ).start()
-            inner_out_value = inner_out[phase, at]
-            sig[at] = inner_out_value + far_in[phase, at]
+            sum_out(phase, chunk).start()
+            sig[at] = inner_out[phase, at] + far_in[phase, at]
+
+    def sum_total(phase, chunk):
+        at, _ = sum_place(phase, chunk)
 
         @pl.when(inner == 0)
         def _():
+            sum_swap(phase, chunk).wait_recv()
             sig[at] = part[phase, at] + far_in[phase, at]
 
     def sum_drain(phase, chunk):
-        at = pl.ds(chunk * CHUNK, CHUNK)
-        index = sum_index(phase, chunk)
-
         @pl.when(inner == 0)
         def _():
-            copy_to(part.at[phase, at], near_in.at[phase, at], far, index).wait_send()
+            sum_in(phase, chunk).wait_send()
 
         @pl.when(inner == 1)
         def _():
-            copy_to(inner_out.at[phase, at], far_in.at[phase, at], far, index + 1).wait_send()
-            copy_to(outer_out.at[phase, at], far_in.at[phase, at], near, index + 2).wait_send()
-
-    state["sum"] = 0
-    state["next"] = 2 * 3 * (256 // CHUNK)
-    chunks = range(256 // CHUNK)
+            sum_swap(phase, chunk).wait_send()
+            sum_out(phase, chunk).wait_send()
+
+    state["next"] = 2 * 3 * len(CHUNKS)
+    chunks = range(len(CHUNKS))
     plain = (((1,), (0,)), ((), ()))
     turned = (((1,), (1,)), ((), ()))
 
-    load_acts.wait()
-    to_plane, own_first = start_gather(acts)
-    load_enc.wait()
-    swap_enc = send(wenc.at[0], wenc.at[1], sibling)
-    load_dec.wait()
-    swap_dec = send(wdec.at[0], wdec.at[1], sibling)
-    bias[:, 0:256] = benc_ref[0:1, :]
-    swap_bias = send(bias.at[:, pl.ds(0, 256)], bias.at[:, pl.ds(256, 256)], sibling)
-    wait_all(own_first)
-    own_second = gather_second(acts, 0)
-    split_weights(0)
-    to_plane.wait_recv()
-    other_first = gather_first(acts, 1)
-    own_rest = gather_forward(acts, 0, own_second)
-    swap_enc.wait_recv()
-    split_weights(1)
-    wait_all(other_first)
-    other_second = gather_second(acts, 1)
-    wait_all(own_rest)
-
     def encode(chunk):
-        at = pl.ds(chunk * CHUNK, CHUNK)
+        at, _ = sum_place(0, chunk)
         part[0, at] = product(acts[at], wenc_h[...], wenc_l[...], plain)
         sum_start(0, chunk)
 
-    encode(0)
-    encode(1)
-    split_decoder(0)
-    other_rest = gather_forward(acts, 1, other_second)
-    sum_middle(0, 0)
-    sum_middle(0, 1)
-    swap_dec.wait_recv()
-    split_decoder(1)
-    wait_all(other_rest)
-    encode(2)
-    encode(3)
-    give_acts = send(acts, acts_sib, sibling)
-    swap_bias.wait_recv()
-    sum_middle(0, 2)
-    sum_middle(0, 3)
-
     def decode(chunk):
-        at = pl.ds(chunk * CHUNK, CHUNK)
-        sum_finish(0, chunk)
+        sum_total(0, chunk)
+        at, _ = sum_place(0, chunk)
+        count = CHUNKS[chunk][1]
         codes, gate = softplus_and_sigmoid(sig[at] + bias[...])
-        sig[at] = gate
+        pg[at] = gate
         high, low = split(codes)
         both = jnp.concatenate([high, low], axis=0)
         for block in range(3):
             cols = slice(block * 768, (block + 1) * 768)
             main = jnp.dot(both, wdec_h[:, cols], preferred_element_type=F32)
             cross = jnp.dot(high, wdec_l[:, cols], preferred_element_type=F32)
-            recon[at, cols] = main[:CHUNK] + (main[CHUNK:] + cross)
+            recon[at, cols] = main[:count] + (main[count:] + cross)
 
     half = 2 * UNIT
 
-    def scatter_start(plane):
+    def scatter_near(plane):
+        up1 = send(rows(recon, row(plane, 1, 0) + half, half), from_down.at[plane, pl.ds(half, half)], second(1))
+        down0 = send(rows(recon, row(plane, 2, 0), half), from_up.at[plane, pl.ds(0, half)], second(-1))
+        return up1, down0
+
+    def scatter_far(plane):
         base = row(plane, 3, 0)
         a = send(rows(recon, base, half), far_a.at[plane], second(1))
         b = send(rows(recon, base + half, half), far_b.at[plane], second(-1))
-        up1 = send(rows(recon, row(plane, 1, 0) + half, half), from_down.at[plane, pl.ds(half, half)], second(1))
-        down0 = send(rows(recon, row(plane, 2, 0), half), from_up.at[plane, pl.ds(0, half)], second(-1))
-        return a, b, up1, down0
+        return a, b
 
     def scatter_add(plane, copies):
-        a, b, up1, down0 = copies
+        a, b = copies
         to_up = pl.ds(row(plane, 1, 0), half)
         to_down = pl.ds(row(plane, 2, 0) + half, half)
         a.wait_recv()
@@ -358,7 +336,7 @@
         b.wait_recv()
         recon[to_down] = recon[to_down] + far_b[plane]
         down1 = send(recon.at[to_down], from_up.at[plane, pl.ds(half, half)], second(-1))
-        return up1, down0, up0, down1
+        return up0, down1
 
     def scatter_first(plane, copies):
         wait_all(copies)
@@ -373,93 +351,172 @@
         wait_all(copies)
         return row_sum[plane, 0:UNIT] + (first_in[plane, 0] + (first_in[plane, 1] + first_in[plane, 2]))
 
+    def residual(plane, total):
+        at = pl.ds(row(plane, 0, 0), UNIT)
+        resid[at] = total + bdec_ref[...] - acts[at]
+
+    def code_gradient(chunk):
+        at, _ = sum_place(1, chunk)
+        part[1, at] = product(resid[at], wdec_h[...], wdec_l[...], turned) + norms[0:1, :]
+        sum_start(1, chunk)
+
+    def turn(i, _):
+        cols = pl.ds(pl.multiple_of(i * 256, 256), 256)
+        for plane in range(2):
+            for side, ref in enumerate((acts, acts_sib)):
+                to = (plane * 2 + side) * 128
+                high, low = split(jnp.transpose(ref[plane * 128 : (plane + 1) * 128, cols]))
+                acts_th[cols, to : to + 128] = high
+                acts_tl[cols, to : to + 128] = low
+        return 0
+
+    gives = {}
+
+    def finish(chunk):
+        sum_total(1, chunk)
+        at, _ = sum_place(1, chunk)
+        pg[at] = pg[at] * sig[at]
+        gives[chunk] = send(pg.at[at, pl.ds(256, 256)], pg_in.at[at], sibling)
+
+    def gradient(plane):
+        at = slice(plane * 128, (plane + 1) * 128)
+        right_h, right_l = split(jnp.concatenate([pg[at, 0:256], pg_in[at, :]], axis=0))
+        cols = slice(plane * 256, (plane + 1) * 256)
+
+        def block(i):
+            high = acts_th[i * 256 : (i + 1) * 256, cols]
+            low = acts_tl[i * 256 : (i + 1) * 256, cols]
+            main = jnp.dot(high, right_h, preferred_element_type=F32)
+            cross = jnp.dot(high, right_l, preferred_element_type=F32) + jnp.dot(low, right_h, preferred_element_type=F32)
+            return main + cross
+
+        return block
+
+    load_acts.wait()
+    to_plane, own_first = start_gather(acts)
+    load_enc.wait()
+    swap_enc = send(wenc.at[0], wenc.at[1], sibling)
+    bias[:, 0:256] = benc_ref[0:1, :]
+    swap_bias = send(bias.at[:, pl.ds(0, 256)], bias.at[:, pl.ds(256, 256)], sibling)
+    split_weights(0)
+    wait_all(own_first)
+    own_second = gather_second(acts, 0)
+    load_dec.wait()
+    swap_dec = send(wdec.at[0], wdec.at[1], sibling)
+    to_plane.wait_recv()
+    other_first = gather_first(acts, 1)
+    swap_enc.wait_recv()
+    split_weights(1)
+    encode(0)
+    own_rest = gather_forward(acts, 0, own_second)
+    wait_all(other_first)
+    other_second = gather_second(acts, 1)
+    wait_all(own_rest[:2])
+    encode(1)
+    sum_middle(0, 0)
+    other_rest = gather_forward(acts, 1, other_second)
+    wait_all(own_rest[2:])
+    encode(2)
+    sum_middle(0, 1)
+    encode(3)
+    sum_relay(0, 0)
+    wait_all(other_rest[:2])
+    encode(4)
+    sum_middle(0, 2)
+    sum_relay(0, 1)
+    split_decoder(0)
+    wait_all(other_rest[2:])
+    encode(5)
+    sum_middle(0, 3)
+    sum_relay(0, 2)
+    swap_dec.wait_recv()
+    split_decoder(1)
+    sum_middle(0, 4)
+    swap_bias.wait_recv()
+    sum_relay(0, 3)
+    sum_middle(0, 5)
+
     decode(0)
+    sum_relay(0, 4)
     decode(1)
-    own_scatter = scatter_start(0)
+    own_near = scatter_near(0)
     decode(2)
-    own_scatter = scatter_add(0, own_scatter)
+    own_far = scatter_far(0)
+    sum_relay(0, 5)
+    give_acts = send(acts, acts_sib, sibling)
     decode(3)
-    other_scatter = scatter_start(1)
-    own_scatter = scatter_first(0, own_scatter)
-    other_scatter = scatter_add(1, other_scatter)
-    other_scatter = scatter_first(1, other_scatter)
+    decode(4)
+    other_near = scatter_near(1)
+    own_near = own_near + scatter_add(0, own_far)
+    decode(5)
+    other_far = scatter_far(1)
+    own_scatter = scatter_first(0, own_near)
+    other_near = other_near + scatter_add(1, other_far)
     plane_out[0] = scatter_total(0, own_scatter)
     own_to_plane = send(plane_out.at[0], plane_in.at[0], other_plane)
+    other_scatter = scatter_first(1, other_near)
+    give_acts.wait_recv()
+    lax.fori_loop(0, 3, turn, 0)
     other_total = scatter_total(1, other_scatter)
     plane_out[1] = other_total
     other_to_plane = send(plane_out.at[1], plane_in.at[1], other_plane)
 
-    def residual(plane, total):
-        at = pl.ds(row(plane, 0, 0), UNIT)
-        resid[at] = total + bdec_ref[...] - acts[at]
-
-    def turn(i, _):
-        cols = pl.ds(pl.multiple_of(i * 256, 256), 256)
-        for half_at, ref in ((0, acts), (256, acts_sib)):
-            high, low = split(jnp.transpose(ref[:, cols]))
-            acts_th[cols, half_at : half_at + 256] = high
-            acts_tl[cols, half_at : half_at + 256] = low
-        return 0
-
     own_to_plane.wait_recv()
     residual(1, other_total + plane_in[0])
     other_first = gather_first(resid, 1)
-    give_acts.wait_recv()
-    lax.fori_loop(0, 4, turn, 0)
+    lax.fori_loop(3, 9, turn, 0)
     wait_all(other_first)
     other_second = gather_second(resid, 1)
-    lax.fori_loop(4, 6, turn, 0)
     other_to_plane.wait_recv()
     residual(0, plane_out[0] + plane_in[1])
     own_first = gather_first(resid, 0)
+    code_gradient(3)
     other_rest = gather_forward(resid, 1, other_second)
-    lax.fori_loop(6, 9, turn, 0)
     wait_all(own_first)
     own_second = gather_second(resid, 0)
-    wait_all(other_rest)
-
-    def code_gradient(chunk):
-        at = pl.ds(chunk * CHUNK, CHUNK)
-        part[1, at] = product(resid[at], wdec_h[...], wdec_l[...], turned) + norms[0:1, :]
-        sum_start(1, chunk)
-
-    pre_sig = pg
-    pre_sig[...] = sig[...]
+    wait_all(other_rest[:2])
+    code_gradient(4)
+    sum_middle(1, 3)
+    own_rest = gather_forward(resid, 0, own_second)
+    wait_all(other_rest[2:])
+    code_gradient(5)
+    sum_middle(1, 4)
+    code_gradient(0)
+    sum_relay(1, 3)
+    sum_middle(1, 5)
+    wait_all(own_rest[:2])
+    code_gradient(1)
+    sum_relay(1, 4)
+    sum_middle(1, 0)
+    wait_all(own_rest[2:])
     code_gradient(2)
-    code_gradient(3)
-    own_rest = gather_forward(resid, 0, own_second)
+    sum_relay(1, 5)
+    sum_middle(1, 1)
+    sum_relay(1, 0)
+    finish(3)
+    finish(4)
     sum_middle(1, 2)
-    sum_middle(1, 3)
-    wait_all(own_rest)
-    code_gradient(0)
-    code_gradient(1)
-    sum_middle(1, 0)
-    sum_middle(1, 1)
-    gives = []
-    for chunk in (2, 3, 0, 1):
-        at = pl.ds(chunk * CHUNK, CHUNK)
-        sum_finish(1, chunk)
-        pg[at] = pg[at] * sig[at]
-        gives.append(send(pg.at[at, pl.ds(256, 256)], pg_in.at[at], sibling))
-    wait_all(gives)
-
-    mine = pg[:, 0:256]
-    theirs = pg_in[...]
-    gbias_ref[...] = jnp.sum(mine, axis=0, keepdims=True) + jnp.sum(theirs, axis=0, keepdims=True)
-    right_h, right_l = split(jnp.concatenate([mine, theirs], axis=0))
-
+    finish(5)
+    sum_relay(1, 1)
+    finish(0)
+    wait_all([gives[3], gives[4], gives[5]])
+    block = gradient(1)
+    for i in range(9):
+        grad_buf[i * 256 : (i + 1) * 256, :] = block(i)
+    sum_relay(1, 2)
+    finish(1)
+    finish(2)
+    wait_all([gives[0], gives[1], gives[2]])
+
+    block = gradient(0)
     stores = []
     for i in range(9):
         at = pl.ds(i * 256, 256)
-        high = acts_th[at, :]
-        main = jnp.dot(high, right_h, preferred_element_type=F32)
-        cross = jnp.dot(high, right_l, preferred_element_type=F32) + jnp.dot(
-            acts_tl[at, :], right_h, preferred_element_type=F32
-        )
-        grad_buf[at, :] = main + cross
+        grad_buf[at, :] = grad_buf[at, :] + block(i)
         store = pltpu.make_async_copy(grad_buf.at[at], grad_hbm.at[0, at], lsem.at[3 + i])
         store.start()
         stores.append(store)
+    gbias_ref[...] = jnp.sum(pg[:, 0:256], axis=0, keepdims=True) + jnp.sum(pg_in[...], axis=0, keepdims=True)
 
     for copy in sent:
         copy.wait_send()
@@ -474,7 +531,7 @@
     depth = acts.shape[2]
     any_space = pl.BlockSpec(memory_space=pl.ANY)
     vmem = pl.BlockSpec(memory_space=pltpu.VMEM)
-    copies = 110
+    copies = 120
     grad, bias = pl.pallas_call(
         kernel,
         out_shape=(

time: 126 us -> 111 us (0.88)
  Pallas kernels: 122 us -> 107 us
    pallas_call x1, Pallas kernels: 122 us -> 107 us  [on_device(): pl.pallas_call(kernel, out_shape=(jax.ShapeDtypeStruct((1, depth, 256), F...]
where the time goes in v3:
time: 111 us
  Pallas kernels  107 us (96%)
  local copies, waits for them, and re-layouts  3.79 us (3%)
    pallas_call x1, Pallas kernels, on_device(): pl.pallas_call(kernel, out_shape=(jax.ShapeDtypeStruct((1, depth, 256), F...  107 us
    unnamed x4, local copies, waits for them, and re-layouts  3.79 us

profile of v3, /device:TPU:1, one launch (start us, length us, event | category | flops | bytes accessed | tf_op | source)
XLA Modules:
  0.0 111.2 jit_solution(5304211477824576115)
XLA Ops:
  0.6 106.8 %crosscoder_gradient.1 = (f32[1,2304,256]{2,1,0:T(8,128)}, f32[1,256]{1,0:T(1,128)}) custom-call(f32[1,8,2304]{2,1,0:T(8,128)} %acts_hbm.1, f32[1,2304,256]{2,1,0:T(8,128)} %wenc_hbm.1, f32[256,1,2304]{2,1,0:T(1,128)} %wdec_hbm.1, f32[1,2304]{1,0:T(1,128)} %bdec_ref.1, f32[1,256]{1,0:T(1,128)} %bitcast.3), custom_call_target="tpu_custom_call" | custom-call | flops 7299999744 | bytes 10000000 | tf_op jit(solution)/shard_map/crosscoder_gradient/pallas_call | solution.py:535
  107.4 0.0 copy-start
  107.4 3.2 %copy.9 = f32[1,2304,256]{2,1,0:T(8,128)} copy(f32[1,2304,256]{2,1,0:T(8,128)} %get-tuple-element.8) | data formatting | bytes 4718592
  110.6 0.0 copy-done
  110.6 0.6 copy.10
Async XLA Ops:
  107.4 3.2 %copy-start = (f32[1,256]{1,0:T(1,128)S(1)}, f32[1,256]{1,0:T(1,128)}, u32[]{:S(2)}) copy-start(f32[1,256]{1,0:T(1,128)} %get-tuple-element.5) | copy-start | bytes 3076

commit v4 on v3

--- a/solution.py
+++ b/solution.py
@@ -14,7 +14,8 @@
 
 STEPS = (0, 1, -1, 2)
 UNIT = 8
-CHUNKS = ((0, 32), (32, 64), (96, 32), (128, 32), (160, 64), (224, 32))
+PIECE = 32
+PIECES = 8
 
 
 def split(value):
@@ -68,6 +69,8 @@
     pg_in,
     acts_th,
     acts_tl,
+    wdec_th,
+    wdec_tl,
     grad_buf,
     ssem,
     rsem,
@@ -217,16 +220,15 @@
         )
         norms[:, slot * 256 : (slot + 1) * 256] = jnp.sqrt(total)
 
-    def product(left, right_h, right_l, dims):
+    def product(left, right_h, right_l):
         high, low = split(left)
         count = left.shape[0]
-        both = lax.dot_general(jnp.concatenate([high, low], axis=0), right_h, dims, preferred_element_type=F32)
-        cross = lax.dot_general(high, right_l, dims, preferred_element_type=F32)
+        both = lax.dot_general(jnp.concatenate([high, low], axis=0), right_h, plain, preferred_element_type=F32)
+        cross = lax.dot_general(high, right_l, plain, preferred_element_type=F32)
         return both[:count] + (both[count:] + cross)
 
     def sum_place(phase, chunk):
-        start, count = CHUNKS[chunk]
-        return pl.ds(start, count), (phase * len(CHUNKS) + chunk) * 3
+        return pl.ds(chunk * PIECE, PIECE), (phase * PIECES + chunk) * 3
 
     def sum_in(phase, chunk):
         at, index = sum_place(phase, chunk)
@@ -289,20 +291,21 @@
             sum_swap(phase, chunk).wait_send()
             sum_out(phase, chunk).wait_send()
 
-    state["next"] = 2 * 3 * len(CHUNKS)
-    chunks = range(len(CHUNKS))
+    state["next"] = 2 * 3 * PIECES
+    chunks = range(PIECES)
     plain = (((1,), (0,)), ((), ()))
-    turned = (((1,), (1,)), ((), ()))
-
-    def encode(chunk):
-        at, _ = sum_place(0, chunk)
-        part[0, at] = product(acts[at], wenc_h[...], wenc_l[...], plain)
-        sum_start(0, chunk)
-
-    def decode(chunk):
-        sum_total(0, chunk)
-        at, _ = sum_place(0, chunk)
-        count = CHUNKS[chunk][1]
+
+    def encode(chunk, pieces):
+        at = pl.ds(chunk * PIECE, pieces * PIECE)
+        part[0, at] = product(acts[at], wenc_h[...], wenc_l[...])
+        for piece in range(chunk, chunk + pieces):
+            sum_start(0, piece)
+
+    def decode(chunk, pieces):
+        for piece in range(chunk, chunk + pieces):
+            sum_total(0, piece)
+        count = pieces * PIECE
+        at = pl.ds(chunk * PIECE, count)
         codes, gate = softplus_and_sigmoid(sig[at] + bias[...])
         pg[at] = gate
         high, low = split(codes)
@@ -355,10 +358,17 @@
         at = pl.ds(row(plane, 0, 0), UNIT)
         resid[at] = total + bdec_ref[...] - acts[at]
 
-    def code_gradient(chunk):
-        at, _ = sum_place(1, chunk)
-        part[1, at] = product(resid[at], wdec_h[...], wdec_l[...], turned) + norms[0:1, :]
-        sum_start(1, chunk)
+    def code_gradient(chunk, pieces):
+        at = pl.ds(chunk * PIECE, pieces * PIECE)
+        part[1, at] = product(resid[at], wdec_th[...], wdec_tl[...]) + norms[0:1, :]
+        for piece in range(chunk, chunk + pieces):
+            sum_start(1, piece)
+
+    def turn_decoder(i, _):
+        cols = pl.ds(pl.multiple_of(i * 256, 256), 256)
+        wdec_th[cols, :] = jnp.transpose(wdec_h[:, cols])
+        wdec_tl[cols, :] = jnp.transpose(wdec_l[:, cols])
+        return 0
 
     def turn(i, _):
         cols = pl.ds(pl.multiple_of(i * 256, 256), 256)
@@ -400,63 +410,66 @@
     swap_bias = send(bias.at[:, pl.ds(0, 256)], bias.at[:, pl.ds(256, 256)], sibling)
     split_weights(0)
     wait_all(own_first)
+    to_plane.wait_recv()
+    other_first = gather_first(acts, 1)
     own_second = gather_second(acts, 0)
     load_dec.wait()
     swap_dec = send(wdec.at[0], wdec.at[1], sibling)
-    to_plane.wait_recv()
-    other_first = gather_first(acts, 1)
     swap_enc.wait_recv()
     split_weights(1)
-    encode(0)
+    encode(0, 1)
     own_rest = gather_forward(acts, 0, own_second)
     wait_all(other_first)
     other_second = gather_second(acts, 1)
     wait_all(own_rest[:2])
-    encode(1)
+    encode(1, 2)
     sum_middle(0, 0)
+    sum_middle(0, 1)
     other_rest = gather_forward(acts, 1, other_second)
+    sum_middle(0, 2)
     wait_all(own_rest[2:])
-    encode(2)
-    sum_middle(0, 1)
-    encode(3)
+    encode(3, 1)
+    encode(4, 1)
     sum_relay(0, 0)
     wait_all(other_rest[:2])
-    encode(4)
-    sum_middle(0, 2)
+    encode(5, 2)
+    split_decoder(0)
     sum_relay(0, 1)
-    split_decoder(0)
-    wait_all(other_rest[2:])
-    encode(5)
     sum_middle(0, 3)
     sum_relay(0, 2)
+    wait_all(other_rest[2:])
+    encode(7, 1)
+    give_acts = send(acts, acts_sib, sibling)
+    sum_middle(0, 4)
     swap_dec.wait_recv()
     split_decoder(1)
-    sum_middle(0, 4)
+    sum_middle(0, 5)
+    sum_middle(0, 6)
+    sum_relay(0, 3)
     swap_bias.wait_recv()
-    sum_relay(0, 3)
-    sum_middle(0, 5)
-
-    decode(0)
+
+    decode(0, 1)
+    sum_middle(0, 7)
     sum_relay(0, 4)
-    decode(1)
+    decode(1, 2)
     own_near = scatter_near(0)
-    decode(2)
+    sum_relay(0, 5)
+    sum_relay(0, 6)
+    decode(3, 1)
     own_far = scatter_far(0)
-    sum_relay(0, 5)
-    give_acts = send(acts, acts_sib, sibling)
-    decode(3)
-    decode(4)
+    sum_relay(0, 7)
+    decode(4, 1)
+    decode(5, 2)
     other_near = scatter_near(1)
     own_near = own_near + scatter_add(0, own_far)
-    decode(5)
+    decode(7, 1)
     other_far = scatter_far(1)
+    lax.fori_loop(0, 9, turn_decoder, 0)
     own_scatter = scatter_first(0, own_near)
     other_near = other_near + scatter_add(1, other_far)
     plane_out[0] = scatter_total(0, own_scatter)
     own_to_plane = send(plane_out.at[0], plane_in.at[0], other_plane)
     other_scatter = scatter_first(1, other_near)
-    give_acts.wait_recv()
-    lax.fori_loop(0, 3, turn, 0)
     other_total = scatter_total(1, other_scatter)
     plane_out[1] = other_total
     other_to_plane = send(plane_out.at[1], plane_in.at[1], other_plane)
@@ -464,49 +477,52 @@
     own_to_plane.wait_recv()
     residual(1, other_total + plane_in[0])
     other_first = gather_first(resid, 1)
-    lax.fori_loop(3, 9, turn, 0)
-    wait_all(other_first)
-    other_second = gather_second(resid, 1)
+    give_acts.wait_recv()
+    lax.fori_loop(0, 9, turn, 0)
     other_to_plane.wait_recv()
     residual(0, plane_out[0] + plane_in[1])
     own_first = gather_first(resid, 0)
-    code_gradient(3)
+    wait_all(other_first)
+    other_second = gather_second(resid, 1)
+    code_gradient(4, 1)
     other_rest = gather_forward(resid, 1, other_second)
     wait_all(own_first)
     own_second = gather_second(resid, 0)
     wait_all(other_rest[:2])
-    code_gradient(4)
+    code_gradient(5, 2)
+    sum_middle(1, 4)
+    own_rest = gather_forward(resid, 0, own_second)
+    sum_middle(1, 5)
+    sum_middle(1, 6)
+    wait_all(other_rest[2:])
+    code_gradient(7, 1)
+    code_gradient(0, 1)
+    sum_relay(1, 4)
+    wait_all(own_rest[:2])
+    code_gradient(1, 2)
+    sum_middle(1, 7)
+    wait_all(own_rest[2:])
+    code_gradient(3, 1)
+    sum_middle(1, 0)
+    sum_relay(1, 5)
+    sum_relay(1, 6)
+    sum_middle(1, 1)
+    sum_middle(1, 2)
+    sum_relay(1, 7)
     sum_middle(1, 3)
-    own_rest = gather_forward(resid, 0, own_second)
-    wait_all(other_rest[2:])
-    code_gradient(5)
-    sum_middle(1, 4)
-    code_gradient(0)
-    sum_relay(1, 3)
-    sum_middle(1, 5)
-    wait_all(own_rest[:2])
-    code_gradient(1)
-    sum_relay(1, 4)
-    sum_middle(1, 0)
-    wait_all(own_rest[2:])
-    code_gradient(2)
-    sum_relay(1, 5)
-    sum_middle(1, 1)
     sum_relay(1, 0)
-    finish(3)
-    finish(4)
-    sum_middle(1, 2)
-    finish(5)
+    for chunk in (4, 5, 6, 7):
+        finish(chunk)
     sum_relay(1, 1)
-    finish(0)
-    wait_all([gives[3], gives[4], gives[5]])
+    sum_relay(1, 2)
+    wait_all([gives[4], gives[5], gives[6], gives[7]])
     block = gradient(1)
     for i in range(9):
         grad_buf[i * 256 : (i + 1) * 256, :] = block(i)
-    sum_relay(1, 2)
-    finish(1)
-    finish(2)
-    wait_all([gives[0], gives[1], gives[2]])
+    sum_relay(1, 3)
+    for chunk in (0, 1, 2, 3):
+        finish(chunk)
+    wait_all([gives[0], gives[1], gives[2], gives[3]])
 
     block = gradient(0)
     stores = []
@@ -531,7 +547,7 @@
     depth = acts.shape[2]
     any_space = pl.BlockSpec(memory_space=pl.ANY)
     vmem = pl.BlockSpec(memory_space=pltpu.VMEM)
-    copies = 120
+    copies = 140
     grad, bias = pl.pallas_call(
         kernel,
         out_shape=(
@@ -571,6 +587,8 @@
             pltpu.VMEM((256, 256), F32),
             pltpu.VMEM((depth, 512), BF16),
             pltpu.VMEM((depth, 512), BF16),
+            pltpu.VMEM((depth, 512), BF16),
+            pltpu.VMEM((depth, 512), BF16),
             pltpu.VMEM((depth, 256), F32),
             pltpu.SemaphoreType.DMA((copies,)),
             pltpu.SemaphoreType.DMA((copies,)),

time: 111 us -> 108 us (0.973)
  Pallas kernels: 107 us -> 104 us
    pallas_call x1, Pallas kernels: 107 us -> 104 us  [on_device(): pl.pallas_call(kernel, out_shape=(jax.ShapeDtypeStruct((1, depth, 256), F...]
where the time goes in v4:
time: 108 us
  Pallas kernels  104 us (96%)
  local copies, waits for them, and re-layouts  3.79 us (4%)
    pallas_call x1, Pallas kernels, on_device(): pl.pallas_call(kernel, out_shape=(jax.ShapeDtypeStruct((1, depth, 256), F...  104 us
    unnamed x4, local copies, waits for them, and re-layouts  3.79 us

profile of v4, /device:TPU:1, one launch (start us, length us, event | category | flops | bytes accessed | tf_op | source)
XLA Modules:
  0.0 108.1 jit_solution(10515945373069645613)
XLA Ops:
  0.6 103.7 %crosscoder_gradient.1 = (f32[1,2304,256]{2,1,0:T(8,128)}, f32[1,256]{1,0:T(1,128)}) custom-call(f32[1,8,2304]{2,1,0:T(8,128)} %acts_hbm.1, f32[1,2304,256]{2,1,0:T(8,128)} %wenc_hbm.1, f32[256,1,2304]{2,1,0:T(1,128)} %wdec_hbm.1, f32[1,2304]{1,0:T(1,128)} %bdec_ref.1, f32[1,256]{1,0:T(1,128)} %bitcast.3), custom_call_target="tpu_custom_call" | custom-call | flops 7299999744 | bytes 10000000 | tf_op jit(solution)/shard_map/crosscoder_gradient/pallas_call | solution.py:551
  104.3 0.0 copy-start
  104.3 3.2 %copy.9 = f32[1,2304,256]{2,1,0:T(8,128)} copy(f32[1,2304,256]{2,1,0:T(8,128)} %get-tuple-element.8) | data formatting | bytes 4718592
  107.6 0.0 copy-done
  107.6 0.6 copy.10
Async XLA Ops:
  104.3 3.2 %copy-start = (f32[1,256]{1,0:T(1,128)S(1)}, f32[1,256]{1,0:T(1,128)}, u32[]{:S(2)}) copy-start(f32[1,256]{1,0:T(1,128)} %get-tuple-element.5) | copy-start | bytes 3076

commit v5 on v4

--- a/solution.py
+++ b/solution.py
@@ -37,7 +37,9 @@
     wdec_hbm,
     bdec_ref,
     benc_ref,
-    grad_hbm,
+    done_hbm,
+    left_hbm,
+    right_ref,
     gbias_ref,
     acts,
     acts_sib,
@@ -372,12 +374,10 @@
 
     def turn(i, _):
         cols = pl.ds(pl.multiple_of(i * 256, 256), 256)
-        for plane in range(2):
-            for side, ref in enumerate((acts, acts_sib)):
-                to = (plane * 2 + side) * 128
-                high, low = split(jnp.transpose(ref[plane * 128 : (plane + 1) * 128, cols]))
-                acts_th[cols, to : to + 128] = high
-                acts_tl[cols, to : to + 128] = low
+        for side, ref in enumerate((acts, acts_sib)):
+            high, low = split(jnp.transpose(ref[128:256, cols]))
+            acts_th[cols, side * 128 : (side + 1) * 128] = high
+            acts_tl[cols, side * 128 : (side + 1) * 128] = low
         return 0
 
     gives = {}
@@ -387,20 +387,6 @@
         at, _ = sum_place(1, chunk)
         pg[at] = pg[at] * sig[at]
         gives[chunk] = send(pg.at[at, pl.ds(256, 256)], pg_in.at[at], sibling)
-
-    def gradient(plane):
-        at = slice(plane * 128, (plane + 1) * 128)
-        right_h, right_l = split(jnp.concatenate([pg[at, 0:256], pg_in[at, :]], axis=0))
-        cols = slice(plane * 256, (plane + 1) * 256)
-
-        def block(i):
-            high = acts_th[i * 256 : (i + 1) * 256, cols]
-            low = acts_tl[i * 256 : (i + 1) * 256, cols]
-            main = jnp.dot(high, right_h, preferred_element_type=F32)
-            cross = jnp.dot(high, right_l, preferred_element_type=F32) + jnp.dot(low, right_h, preferred_element_type=F32)
-            return main + cross
-
-        return block
 
     load_acts.wait()
     to_plane, own_first = start_gather(acts)
@@ -515,24 +501,33 @@
         finish(chunk)
     sum_relay(1, 1)
     sum_relay(1, 2)
+    stores = []
+
+    def store(src, dst):
+        copy = pltpu.make_async_copy(src, dst, lsem.at[3 + len(stores)])
+        copy.start()
+        stores.append(copy)
+
+    store(acts.at[pl.ds(0, 128)], left_hbm.at[pl.ds(0, 128)])
+    store(acts_sib.at[pl.ds(0, 128)], left_hbm.at[pl.ds(128, 128)])
     wait_all([gives[4], gives[5], gives[6], gives[7]])
-    block = gradient(1)
+    right_h, right_l = split(jnp.concatenate([pg[128:256, 0:256], pg_in[128:256, :]], axis=0))
     for i in range(9):
-        grad_buf[i * 256 : (i + 1) * 256, :] = block(i)
+        at = pl.ds(i * 256, 256)
+        high = acts_th[at, :]
+        cross = jnp.dot(high, right_l, preferred_element_type=F32) + jnp.dot(
+            acts_tl[at, :], right_h, preferred_element_type=F32
+        )
+        grad_buf[at, :] = jnp.dot(high, right_h, preferred_element_type=F32) + cross
+        store(grad_buf.at[at], done_hbm.at[at])
     sum_relay(1, 3)
     for chunk in (0, 1, 2, 3):
         finish(chunk)
+    right_ref[0:128, :] = pg[0:128, 0:256]
+    part_bias = jnp.sum(pg[:, 0:256], axis=0, keepdims=True) + jnp.sum(pg_in[128:256, :], axis=0, keepdims=True)
     wait_all([gives[0], gives[1], gives[2], gives[3]])
-
-    block = gradient(0)
-    stores = []
-    for i in range(9):
-        at = pl.ds(i * 256, 256)
-        grad_buf[at, :] = grad_buf[at, :] + block(i)
-        store = pltpu.make_async_copy(grad_buf.at[at], grad_hbm.at[0, at], lsem.at[3 + i])
-        store.start()
-        stores.append(store)
-    gbias_ref[...] = jnp.sum(pg[:, 0:256], axis=0, keepdims=True) + jnp.sum(pg_in[...], axis=0, keepdims=True)
+    right_ref[128:256, :] = pg_in[0:128, :]
+    gbias_ref[...] = part_bias + jnp.sum(pg_in[0:128, :], axis=0, keepdims=True)
 
     for copy in sent:
         copy.wait_send()
@@ -543,19 +538,70 @@
         store.wait()
 
 
+def last_kernel(
+    done_hbm, left_hbm, right_hbm, bias_hbm, grad_hbm, gbias_hbm, done, left, right, bias, grad, sem_in, sem_out
+):
+    pieces = 3
+    width = left.shape[1] // pieces
+
+    def load(src, dst, index):
+        copy = pltpu.make_async_copy(src, dst, sem_in.at[index])
+        copy.start()
+        return copy
+
+    load_right = load(right_hbm, right, 0)
+    loads = []
+    for i in range(pieces):
+        at = pl.ds(i * width, width)
+        loads.append(
+            (
+                load(left_hbm.at[:, at], left.at[:, at], 2 + i),
+                load(done_hbm.at[at], done.at[at], 2 + pieces + i),
+            )
+        )
+    load_bias = load(bias_hbm, bias, 1)
+    load_right.wait()
+    right_h, right_l = split(right[...])
+    dims = (((0,), (0,)), ((), ()))
+    stores = []
+    for i in range(pieces):
+        loads[i][0].wait()
+        loads[i][1].wait()
+        for k in range(i * width, (i + 1) * width, 256):
+            cols = slice(k, k + 256)
+            high, low = split(left[:, cols])
+            cross = lax.dot_general(high, right_l, dims, preferred_element_type=F32) + lax.dot_general(
+                low, right_h, dims, preferred_element_type=F32
+            )
+            main = lax.dot_general(high, right_h, dims, preferred_element_type=F32)
+            grad[cols, :] = done[cols, :] + (main + cross)
+            at = pl.ds(k, 256)
+            store = pltpu.make_async_copy(grad.at[at], grad_hbm.at[0, at], sem_out.at[len(stores)])
+            store.start()
+            stores.append(store)
+    load_bias.wait()
+    store = pltpu.make_async_copy(bias, gbias_hbm, sem_out.at[len(stores)])
+    store.start()
+    stores.append(store)
+    for store in stores:
+        store.wait()
+
+
 def on_device(acts, w_enc, b_enc, w_dec, b_dec):
     depth = acts.shape[2]
     any_space = pl.BlockSpec(memory_space=pl.ANY)
     vmem = pl.BlockSpec(memory_space=pltpu.VMEM)
     copies = 140
-    grad, bias = pl.pallas_call(
+    done, left, right, bias = pl.pallas_call(
         kernel,
         out_shape=(
-            jax.ShapeDtypeStruct((1, depth, 256), F32),
+            jax.ShapeDtypeStruct((depth, 256), F32),
+            jax.ShapeDtypeStruct((256, depth), F32),
+            jax.ShapeDtypeStruct((256, 256), F32),
             jax.ShapeDtypeStruct((1, 256), F32),
         ),
         in_specs=[any_space, any_space, any_space, vmem, vmem],
-        out_specs=(any_space, vmem),
+        out_specs=(any_space, any_space, vmem, vmem),
         scratch_shapes=[
             pltpu.VMEM((256, depth), F32),
             pltpu.VMEM((256, depth), F32),
@@ -585,14 +631,14 @@
             pltpu.VMEM((256, 512), F32),
             pltpu.VMEM((256, 512), F32),
             pltpu.VMEM((256, 256), F32),
-            pltpu.VMEM((depth, 512), BF16),
-            pltpu.VMEM((depth, 512), BF16),
+            pltpu.VMEM((depth, 256), BF16),
+            pltpu.VMEM((depth, 256), BF16),
             pltpu.VMEM((depth, 512), BF16),
             pltpu.VMEM((depth, 512), BF16),
             pltpu.VMEM((depth, 256), F32),
             pltpu.SemaphoreType.DMA((copies,)),
             pltpu.SemaphoreType.DMA((copies,)),
-            pltpu.SemaphoreType.DMA((12,)),
+            pltpu.SemaphoreType.DMA((16,)),
         ],
         compiler_params=pltpu.CompilerParams(
             collective_id=0, has_side_effects=True, vmem_limit_bytes=60 * 1024 * 1024
@@ -600,6 +646,27 @@
         cost_estimate=pl.CostEstimate(flops=7_300_000_000, bytes_accessed=10_000_000, transcendentals=500_000),
         name="crosscoder_gradient",
     )(acts, w_enc, w_dec, b_dec, b_enc.reshape(1, 256))
+    grad, bias = pl.pallas_call(
+        last_kernel,
+        out_shape=(
+            jax.ShapeDtypeStruct((1, depth, 256), F32),
+            jax.ShapeDtypeStruct((1, 256), F32),
+        ),
+        in_specs=[any_space] * 4,
+        out_specs=(any_space, any_space),
+        scratch_shapes=[
+            pltpu.VMEM((depth, 256), F32),
+            pltpu.VMEM((256, depth), F32),
+            pltpu.VMEM((256, 256), F32),
+            pltpu.VMEM((1, 256), F32),
+            pltpu.VMEM((depth, 256), F32),
+            pltpu.SemaphoreType.DMA((8,)),
+            pltpu.SemaphoreType.DMA((10,)),
+        ],
+        compiler_params=pltpu.CompilerParams(vmem_limit_bytes=60 * 1024 * 1024),
+        cost_estimate=pl.CostEstimate(flops=906_000_000, bytes_accessed=7_400_000, transcendentals=0),
+        name="last_product",
+    )(done, left, right, bias)
     return grad, bias.reshape(256)
 
 

time: 108 us -> 107 us (level)
  local copies, waits for them, and re-layouts: 3.79 us -> 0 us
  Pallas kernels: 104 us -> 106 us
    unnamed x4 -> x0, local copies, waits for them, and re-layouts: 3.79 us -> none
    pallas_call x1 -> x2, Pallas kernels: 104 us -> 106 us  [the longest x1 102 us: on_device(): pl.pallas_call(kernel, out_shape=(jax.ShapeDtypeStruct((depth, 256), F32)...]
where the time goes in v5:
time: 107 us
  Pallas kernels  106 us (99%)
    pallas_call x1, Pallas kernels, on_device(): pl.pallas_call(kernel, out_shape=(jax.ShapeDtypeStruct((depth, 256), F32)...  102 us
    pallas_call x1, Pallas kernels, on_device(): pl.pallas_call(last_kernel, out_shape=(jax.ShapeDtypeStruct((1, depth, 25...  4.03 us

profile of v5, /device:TPU:1, one launch (start us, length us, event | category | flops | bytes accessed | tf_op | source)
XLA Modules:
  0.0 107.0 jit_solution(16934575013366785062)
XLA Ops:
  0.6 102.2 %crosscoder_gradient.1 = (f32[2304,256]{1,0:T(8,128)}, f32[256,2304]{1,0:T(8,128)}, f32[256,256]{1,0:T(8,128)}, f32[1,256]{1,0:T(1,128)}) custom-call(f32[1,8,2304]{2,1,0:T(8,128)} %acts_hbm.1, f32[1,2304,256]{2,1,0:T(8,128)} %wenc_hbm.1, f32[256,1,2304]{2,1,0:T(1,128)} %wdec_hbm.1, f32[1,2304]{1,0:T(1,128)} %bdec_ref.1, f32[1,256]{1,0:T(1,128)} %bitcast.2), custom_call_target="tpu_custom_call" | custom-call | flops 7299999744 | bytes 10000000 | tf_op jit(solution)/shard_map/crosscoder_gradient/pallas_call | solution.py:595
  102.8 4.0 %last_product.1 = (f32[1,2304,256]{2,1,0:T(8,128)}, f32[1,256]{1,0:T(1,128)}) custom-call(f32[2304,256]{1,0:T(8,128)} %get-tuple-element.8.done_hbm, f32[256,2304]{1,0:T(8,128)} %get-tuple-element.9.left_hbm, f32[256,256]{1,0:T(8,128)} %get-tuple-element.10.right_hbm, f32[1,256]{1,0:T(1,128)} %get-tuple-element.11.bias_hbm), custom_call_target="tpu_custom_call" | custom-call | flops 906000000 | bytes 7400000 | tf_op jit(solution)/shard_map/last_product/pallas_call | solution.py:649
